TPU v7x, 32 devices: a whole 2x2x4 slice. The times are simulated.
32 devices in a mesh: dp: 8 (over y, x, core), seq: 4 (over z).
Axes of the slice: x: 2, y: 2, z: 4, core: 2. Of those that a mesh axis runs over, the one named last changes fastest.
Arguments:
- tokens: bfloat16 [32, 512, 768], P('dp', 'seq'), may hold values from -6 to 6
- cotangent: bfloat16 [32, 512, 768], P('dp', 'seq'), may hold values from -6 to 6
- lengths: int32 [32], P('dp'), may hold values from 64 to 512, as said below
- qkv_weight: bfloat16 [1, 768, 2304], P(None, ('dp', 'seq')), may hold values from -0.21875 to 0.21875
- qv_bias: bfloat16 [1, 1536], P(None, ('dp', 'seq')), may hold values from -3 to 3
- out_weight: bfloat16 [1, 768, 768], P(None, ('dp', 'seq')), may hold values from -1.75 to 1.75
- out_bias: bfloat16 [1, 768], P(None, ('dp', 'seq')), may hold values from -3 to 3
- norm_gain: bfloat16 [1, 768], P(None, ('dp', 'seq')), may hold values from 0.5 to 1.5
- norm_shift: bfloat16 [1, 768], P(None, ('dp', 'seq')), may hold values from -3 to 3
- up_weight: bfloat16 [1, 768, 3072], P(None, ('dp', 'seq')), may hold values from -0.21875 to 0.21875
- up_bias: bfloat16 [1, 3072], P(None, ('dp', 'seq')), may hold values from -3 to 3
- down_weight: bfloat16 [1, 3072, 768], P(None, ('dp', 'seq')), may hold values from -0.109375 to 0.109375
- down_bias: bfloat16 [1, 768], P(None, ('dp', 'seq')), may hold values from -3 to 3
- final_gain: bfloat16 [1, 768], P(None, ('dp', 'seq')), may hold values from 0.5 to 1.5
- final_shift: bfloat16 [1, 768], P(None, ('dp', 'seq')), may hold values from -3 to 3
Outputs:
- result: bfloat16 [32, 512, 768], P('dp', 'seq')
- tokens_grad: bfloat16 [32, 512, 768], P('dp', 'seq')
- qkv_weight_grad: float32 [1, 768, 2304], P(None, ('dp', 'seq'))
- qv_bias_grad: float32 [1, 1536], P(None, ('dp', 'seq'))
- out_weight_grad: float32 [1, 768, 768], P(None, ('dp', 'seq'))
- out_bias_grad: float32 [1, 768], P(None, ('dp', 'seq'))
- norm_gain_grad: float32 [1, 768], P(None, ('dp', 'seq'))
- norm_shift_grad: float32 [1, 768], P(None, ('dp', 'seq'))
- up_weight_grad: float32 [1, 768, 3072], P(None, ('dp', 'seq'))
- up_bias_grad: float32 [1, 3072], P(None, ('dp', 'seq'))
- down_weight_grad: float32 [1, 3072, 768], P(None, ('dp', 'seq'))
- down_bias_grad: float32 [1, 768], P(None, ('dp', 'seq'))
- final_gain_grad: float32 [1, 768], P(None, ('dp', 'seq'))
- final_shift_grad: float32 [1, 768], P(None, ('dp', 'seq'))
Inputs may be any that keep to these rules, and one draw needn't show every extreme that they name: `lengths`: some sequence is full and some has exactly one eighth of 512 valid tokens.
All inputs are finite; a program needn't handle non-finite values.
Results may differ from a plain program's by a relative error of at most 0.015.
Values may be sent and summed in bfloat16 or wider, within the bound.
A program may use at most 192 MiB of HBM per device.

v0:
```python
import jax
import jax.numpy as jnp
from jax import lax
from jax.sharding import PartitionSpec as P

HEADS = 12
LAYERS = 1


NEG = -1e30
EPS = 1e-05


def norm_rows(residual, gain_vec, shift_vec):
    centred = residual - jnp.mean(residual, axis=-1, keepdims=True)
    inv_std = lax.rsqrt(jnp.mean(centred * centred, axis=-1, keepdims=True) + EPS)
    normed = centred * inv_std
    return (normed * gain_vec + shift_vec, normed, inv_std)


def norm_back(grad_out, normed, inv_std, gain_vec):
    scaled = grad_out * gain_vec
    return inv_std * (
        scaled
        - jnp.mean(scaled, axis=-1, keepdims=True)
        - normed * jnp.mean(scaled * normed, axis=-1, keepdims=True)
    )


def gelu_exact(value):
    return 0.5 * value * (1.0 + lax.erf(value * 0.7071067811865476))


def gelu_slope(value):
    return (
        0.5 * (1.0 + lax.erf(value * 0.7071067811865476))
        + value * jnp.exp(-0.5 * value * value) * 0.3989422804014327
    )


def matmul(left, right):
    return jnp.dot(left, right, preferred_element_type=jnp.float32)


def dot_rows(left, right):
    return lax.dot_general(
        left, right, (((0,), (0,)), ((), ())), preferred_element_type=jnp.float32
    )


def dot_back(left, right):
    return lax.dot_general(
        left, right, (((1,), (1,)), ((), ())), preferred_element_type=jnp.float32
    )


def per_device(
    tokens,
    cotangent,
    lengths,
    qkv_weight,
    qv_bias,
    out_weight,
    out_bias,
    norm_gain,
    norm_shift,
    up_weight,
    up_bias,
    down_weight,
    down_bias,
    final_gain,
    final_shift,
):
    groups = lax.axis_size("seq")
    seq_here, tok_here, model_width = tokens.shape
    head_count = HEADS
    head_dim = model_width // head_count
    row_count = seq_here * tok_here
    key_count = tok_here * groups
    pair_count = seq_here * head_count // groups
    block_rows = min(512, key_count)
    block_count = key_count // block_rows
    score_scale = head_dim ** (-0.5)
    pair_ids = lax.axis_index("seq") * pair_count + jnp.arange(pair_count, dtype=jnp.int32)
    owners = pair_ids // head_count
    picked = owners[:, None] == jnp.arange(seq_here, dtype=jnp.int32)[None, :]
    pair_len = jnp.sum(jnp.where(picked, lengths[None, :], 0), axis=1)
    valid = jnp.arange(key_count, dtype=jnp.int32)[None, :] < pair_len[:, None]

    def to_heads(table, parts):
        shaped = table.reshape(seq_here, tok_here, parts, head_count, head_dim).transpose(
            0, 3, 1, 2, 4
        )
        return shaped.reshape(seq_here * head_count, tok_here, parts * head_dim)

    def from_heads(table, parts):
        shaped = table.reshape(seq_here, head_count, tok_here, parts, head_dim).transpose(
            0, 2, 3, 1, 4
        )
        return shaped.reshape(row_count, parts * model_width)

    def to_blocks(table):
        return table.reshape(pair_count, block_count, block_rows, table.shape[-1]).transpose(
            1, 0, 2, 3
        )

    def from_blocks(table):
        return table.transpose(1, 0, 2, 3).reshape(pair_count, key_count, table.shape[-1])

    def block_scores(q_block, keys_here):
        scores = (
            jnp.einsum("pqd,pkd->pqk", q_block, keys_here, preferred_element_type=jnp.float32)
            * score_scale
        )
        return jnp.where(valid[:, None, :], scores, NEG)

    hidden = tokens.reshape(row_count, model_width).astype(jnp.float32)
    kept_params = []
    current = 0
    params = (
        lax.all_gather(qkv_weight[current], ("dp", "seq"), axis=0, tiled=True),
        lax.all_gather(qv_bias[current], ("dp", "seq"), axis=0, tiled=True),
        lax.all_gather(out_weight[current], ("dp", "seq"), axis=0, tiled=True),
        lax.all_gather(out_bias[current], ("dp", "seq"), axis=0, tiled=True),
        lax.all_gather(norm_gain[current], ("dp", "seq"), axis=0, tiled=True),
        lax.all_gather(norm_shift[current], ("dp", "seq"), axis=0, tiled=True),
        lax.all_gather(up_weight[current], ("dp", "seq"), axis=0, tiled=True),
        lax.all_gather(up_bias[current], ("dp", "seq"), axis=0, tiled=True),
        lax.all_gather(down_weight[current], ("dp", "seq"), axis=0, tiled=True),
        lax.all_gather(down_bias[current], ("dp", "seq"), axis=0, tiled=True),
        lax.all_gather(final_gain[current], ("dp", "seq"), axis=0, tiled=True),
        lax.all_gather(final_shift[current], ("dp", "seq"), axis=0, tiled=True),
    )
    kept_params.append(None)
    (
        mix_w,
        mix_b,
        proj_w,
        proj_b,
        gain_one,
        shift_one,
        upper_w,
        upper_b,
        lower_w,
        lower_b,
        gain_two,
        shift_two,
    ) = params
    hid_half = hidden.astype(jnp.bfloat16)
    bias_full = jnp.concatenate(
        [
            mix_b[:model_width].astype(jnp.float32),
            jnp.zeros((model_width,), jnp.float32),
            mix_b[model_width:].astype(jnp.float32),
        ]
    )
    mixed = (matmul(hid_half, mix_w) + bias_full).astype(jnp.bfloat16)
    by_heads = lax.all_to_all(to_heads(mixed, 3), "seq", split_axis=0, concat_axis=1, tiled=True)
    queries = by_heads[..., :head_dim]
    keys_here = by_heads[..., head_dim : 2 * head_dim]
    values = by_heads[..., 2 * head_dim :]

    def one_block(q_block):
        scores = block_scores(q_block, keys_here)
        row_max = jnp.max(scores, axis=-1, keepdims=True)
        log_total = row_max + jnp.log(jnp.sum(jnp.exp(scores - row_max), axis=-1, keepdims=True))
        attn_probs = jnp.exp(scores - log_total).astype(jnp.bfloat16)
        context = jnp.einsum(
            "pqk,pkd->pqd", attn_probs, values, preferred_element_type=jnp.float32
        ).astype(jnp.bfloat16)
        return (context, log_total[..., 0])

    context, log_total = lax.map(one_block, to_blocks(queries))
    context, log_total = (
        from_blocks(context),
        log_total.transpose(1, 0, 2).reshape(pair_count, key_count),
    )
    context_tok = from_heads(
        lax.all_to_all(context, "seq", split_axis=1, concat_axis=0, tiled=True), 1
    )
    attn_out = matmul(context_tok, proj_w) + proj_b.astype(jnp.float32)
    first_norm, normed_one, inv_one = norm_rows(
        hidden + attn_out, gain_one.astype(jnp.float32), shift_one.astype(jnp.float32)
    )
    first_half = first_norm.astype(jnp.bfloat16)
    pre_act = matmul(first_half, upper_w) + upper_b.astype(jnp.float32)
    activated = gelu_exact(pre_act).astype(jnp.bfloat16)
    mlp_out = matmul(activated, lower_w) + lower_b.astype(jnp.float32)
    hidden, normed_two, inv_two = norm_rows(
        first_norm + mlp_out, gain_two.astype(jnp.float32), shift_two.astype(jnp.float32)
    )
    tapes = [
        (
            hid_half,
            queries,
            keys_here,
            values,
            context,
            log_total,
            context_tok,
            normed_one,
            inv_one,
            first_half,
            pre_act,
            activated,
            normed_two,
            inv_two,
        )
    ]
    output = hidden.astype(jnp.bfloat16).reshape(tokens.shape)
    grad = cotangent.reshape(row_count, model_width).astype(jnp.float32)
    shares = [None] * LAYERS
    for current in reversed(range(LAYERS)):
        params = (
            lax.all_gather(qkv_weight[current], ("dp", "seq"), axis=0, tiled=True),
            lax.all_gather(qv_bias[current], ("dp", "seq"), axis=0, tiled=True),
            lax.all_gather(out_weight[current], ("dp", "seq"), axis=0, tiled=True),
            lax.all_gather(out_bias[current], ("dp", "seq"), axis=0, tiled=True),
            lax.all_gather(norm_gain[current], ("dp", "seq"), axis=0, tiled=True),
            lax.all_gather(norm_shift[current], ("dp", "seq"), axis=0, tiled=True),
            lax.all_gather(up_weight[current], ("dp", "seq"), axis=0, tiled=True),
            lax.all_gather(up_bias[current], ("dp", "seq"), axis=0, tiled=True),
            lax.all_gather(down_weight[current], ("dp", "seq"), axis=0, tiled=True),
            lax.all_gather(down_bias[current], ("dp", "seq"), axis=0, tiled=True),
            lax.all_gather(final_gain[current], ("dp", "seq"), axis=0, tiled=True),
            lax.all_gather(final_shift[current], ("dp", "seq"), axis=0, tiled=True),
        )
        (
            mix_w,
            mix_b,
            proj_w,
            proj_b,
            gain_one,
            shift_one,
            upper_w,
            upper_b,
            lower_w,
            lower_b,
            gain_two,
            shift_two,
        ) = params
        (
            hid_half,
            queries,
            keys_here,
            values,
            context,
            log_total,
            context_tok,
            normed_one,
            inv_one,
            first_half,
            pre_act,
            activated,
            normed_two,
            inv_two,
        ) = tapes[current]
        d_gain_two = jnp.sum(grad * normed_two, axis=0)
        d_shift_two = jnp.sum(grad, axis=0)
        d_second = norm_back(grad, normed_two, inv_two, gain_two.astype(jnp.float32))
        d_second_half = d_second.astype(jnp.bfloat16)
        d_lower_b = jnp.sum(d_second, axis=0)
        d_lower_w = dot_rows(activated, d_second_half)
        d_pre = dot_back(d_second_half, lower_w) * gelu_slope(pre_act)
        d_pre_half = d_pre.astype(jnp.bfloat16)
        d_upper_b = jnp.sum(d_pre, axis=0)
        d_upper_w = dot_rows(first_half, d_pre_half)
        d_first = d_second + dot_back(d_pre_half, upper_w)
        d_gain_one = jnp.sum(d_first * normed_one, axis=0)
        d_shift_one = jnp.sum(d_first, axis=0)
        d_resid = norm_back(d_first, normed_one, inv_one, gain_one.astype(jnp.float32))
        d_resid_half = d_resid.astype(jnp.bfloat16)
        d_proj_b = jnp.sum(d_resid, axis=0)
        d_proj_w = dot_rows(context_tok, d_resid_half)
        d_context = dot_back(d_resid_half, proj_w).astype(jnp.bfloat16)
        d_ctx_heads = lax.all_to_all(
            to_heads(d_context, 1), "seq", split_axis=0, concat_axis=1, tiled=True
        )
        totals_blocks = log_total.reshape(pair_count, block_count, block_rows).transpose(1, 0, 2)

        def attend_one_block(running, pieces):
            q_block, o_block, do_block, lse_block = pieces
            scores = block_scores(q_block, keys_here)
            attn_probs = jnp.exp(scores - lse_block[..., None])
            probs_half = attn_probs.astype(jnp.bfloat16)
            d_values = running[1] + jnp.einsum(
                "pqk,pqd->pkd", probs_half, do_block, preferred_element_type=jnp.float32
            )
            d_probs = jnp.einsum(
                "pqd,pkd->pqk", do_block, values, preferred_element_type=jnp.float32
            )
            delta = jnp.sum(
                do_block.astype(jnp.float32) * o_block.astype(jnp.float32), axis=-1, keepdims=True
            )
            d_scores = (attn_probs * (d_probs - delta) * score_scale).astype(jnp.bfloat16)
            d_queries = jnp.einsum(
                "pqk,pkd->pqd", d_scores, keys_here, preferred_element_type=jnp.float32
            ).astype(jnp.bfloat16)
            d_keys = running[0] + jnp.einsum(
                "pqk,pqd->pkd", d_scores, q_block, preferred_element_type=jnp.float32
            )
            return ((d_keys, d_values), d_queries)

        zero_init = jnp.zeros((pair_count, key_count, head_dim), jnp.float32)
        (d_keys, d_values), d_queries = lax.scan(
            attend_one_block,
            (zero_init, zero_init),
            (to_blocks(queries), to_blocks(context), to_blocks(d_ctx_heads), totals_blocks),
        )
        d_mixed_heads = jnp.concatenate(
            [from_blocks(d_queries), d_keys.astype(jnp.bfloat16), d_values.astype(jnp.bfloat16)],
            axis=-1,
        )
        d_mixed = from_heads(
            lax.all_to_all(d_mixed_heads, "seq", split_axis=1, concat_axis=0, tiled=True), 3
        )
        col_sums = jnp.sum(d_mixed.astype(jnp.float32), axis=0)
        d_mix_b = jnp.concatenate([col_sums[:model_width], col_sums[2 * model_width :]])
        d_mix_w = dot_rows(hid_half, d_mixed)
        grad = d_resid + dot_back(d_mixed, mix_w)
        partials = (
            d_mix_w,
            d_mix_b,
            d_proj_w,
            d_proj_b,
            d_gain_one,
            d_shift_one,
            d_upper_w,
            d_upper_b,
            d_lower_w,
            d_lower_b,
            d_gain_two,
            d_shift_two,
        )
        flats = tuple((item.reshape(-1) for item in partials))
        summed = (
            lax.psum_scatter(flats[0], ("dp", "seq"), scatter_dimension=0, tiled=True),
            lax.psum_scatter(flats[1], ("dp", "seq"), scatter_dimension=0, tiled=True),
            lax.psum_scatter(flats[2], ("dp", "seq"), scatter_dimension=0, tiled=True),
            lax.psum_scatter(flats[3], ("dp", "seq"), scatter_dimension=0, tiled=True),
            lax.psum_scatter(flats[4], ("dp", "seq"), scatter_dimension=0, tiled=True),
            lax.psum_scatter(flats[5], ("dp", "seq"), scatter_dimension=0, tiled=True),
            lax.psum_scatter(flats[6], ("dp", "seq"), scatter_dimension=0, tiled=True),
            lax.psum_scatter(flats[7], ("dp", "seq"), scatter_dimension=0, tiled=True),
            lax.psum_scatter(flats[8], ("dp", "seq"), scatter_dimension=0, tiled=True),
            lax.psum_scatter(flats[9], ("dp", "seq"), scatter_dimension=0, tiled=True),
            lax.psum_scatter(flats[10], ("dp", "seq"), scatter_dimension=0, tiled=True),
            lax.psum_scatter(flats[11], ("dp", "seq"), scatter_dimension=0, tiled=True),
        )
        shares[current] = tuple(
            (piece.reshape((-1,) + whole.shape[1:]) for piece, whole in zip(summed, partials))
        )
    input_grad = grad.astype(jnp.bfloat16).reshape(tokens.shape)
    stacked = tuple((jnp.stack([shares[0][slot]]) for slot in range(12)))
    return (output, input_grad) + stacked


def solution(mesh):
    placed = (
        P("dp", "seq", None),
        P("dp", "seq", None),
        P("dp"),
        P(None, ("dp", "seq"), None),
        P(None, ("dp", "seq")),
        P(None, ("dp", "seq"), None),
        P(None, ("dp", "seq")),
        P(None, ("dp", "seq")),
        P(None, ("dp", "seq")),
        P(None, ("dp", "seq"), None),
        P(None, ("dp", "seq")),
        P(None, ("dp", "seq"), None),
        P(None, ("dp", "seq")),
        P(None, ("dp", "seq")),
        P(None, ("dp", "seq")),
    )
    return jax.shard_map(
        per_device,
        mesh=mesh,
        in_specs=placed,
        out_specs=(
            P("dp", "seq", None),
            P("dp", "seq", None),
            P(None, ("dp", "seq"), None),
            P(None, ("dp", "seq")),
            P(None, ("dp", "seq"), None),
            P(None, ("dp", "seq")),
            P(None, ("dp", "seq")),
            P(None, ("dp", "seq")),
            P(None, ("dp", "seq"), None),
            P(None, ("dp", "seq")),
            P(None, ("dp", "seq"), None),
            P(None, ("dp", "seq")),
            P(None, ("dp", "seq")),
            P(None, ("dp", "seq")),
        ),
        check_vma=False,
    )
```

profile of v0, /device:TPU:0, one launch (start us, length us, event | category | flops | bytes accessed | tf_op | source)
XLA Modules:
  0.0 935.3 jit_solution(7131566736397338918)
XLA Ops:
  10.0 0.8 dynamic-update-slice.7
  16.7 42.5 %all-reduce.22 = (bf16[768]{0:T(1024)(128)(2,1)S(1)}, bf16[1536]{0:T(1024)(128)(2,1)S(1)}, bf16[768]{0:T(1024)(128)(2,1)S(1)}, bf16[768]{0:T(1024)(128)(2,1)S(1)...) all-reduce(bf16[768]{0:T(1024)(128)(2,1)S(1)} %dynamic-update-slice, ...), channel_id=5, replica_groups=mesh['dp'=8,'seq'=4] {'dp','seq'}, use_global_device_ids=true, to_apply=%add.1 | all-reduce | flops 9216 | bytes 36864
  59.2 14.4 %all-gather.17.cloned.1.call-done = bf16[1,768,2304]{2,1,0:T(8,128)(2,1)} async-done(((bf16[1,24,2304]{2,1,0:T(8,128)(2,1)}), bf16[1,768,2304]{2,1,0:T(8,128)(2,1)}) %all-gather.17.cloned.1.call-update) | async-done | bytes 3538960 | tf_op jit(solution)/shard_map/all_gather | solution.py:121
  73.7 5.7 fusion.14
  79.4 2.8 copy.98
  82.2 2.2 reshape.198
  84.4 3.7 copy.99
  88.0 3.8 all-to-all-start
  92.0 58.2 %all-to-all-done = bf16[48,128,192]{1,2,0:T(8,128)(2,1)S(1)} async-done(((bf16[48,128,192]{1,2,0:T(8,128)(2,1)}), bf16[48,128,192]{1,2,0:T(8,128)(2,1)S(1)}, u32[]{:S(2)}, u32[]{:S(2)}) %all-to-all-start) | async-done | bytes 2359328 | tf_op jit(solution)/shard_map/all_to_all | solution.py:158
  150.2 1.4 copy-done.1
  151.6 2.1 copy.161
  153.7 4.5 fusion.1
  158.2 3.0 exponential_reduce_fusion
  161.2 1.6 copy-done
  162.7 3.9 convolution_convert_fusion.2
  166.7 0.9 copy-done.10
  167.5 2.8 copy.102
  170.3 4.2 reshape.271
  174.5 4.4 all-to-all-start.1
  179.3 25.9 %all-to-all-done.1 = bf16[4,2,49152]{2,1,0:T(2,128)(2,1)} async-done(((bf16[4,2,49152]{2,1,0:T(2,128)(2,1)}), bf16[4,2,49152]{2,1,0:T(2,128)(2,1)}, u32[]{:S(2)}, u32[]{:S(2)}) %all-to-all-start.1) | async-done | bytes 786464 | tf_op jit(solution)/shard_map/all_to_all | solution.py:179
  205.2 4.2 reshape.272
  209.4 3.5 copy.103
  212.9 2.7 fusion.80
  215.6 1.2 copy-done.5
  217.1 10.7 %all-gather.21.cloned.1.call-done = bf16[1,768,3072]{2,1,0:T(8,128)(2,1)} async-done(((bf16[1,24,3072]{2,1,0:T(8,128)(2,1)}), bf16[1,768,3072]{2,1,0:T(8,128)(2,1)}) %all-gather.21.cloned.1.call-update) | async-done | bytes 4718608 | tf_op jit(solution)/shard_map/all_gather | solution.py:127
  227.8 8.4 multiply_convert_fusion.1
  236.2 56.2 %all-gather.23.cloned.1.call-done = bf16[1,3072,768]{2,1,0:T(8,128)(2,1)} async-done(((bf16[1,96,768]{2,1,0:T(8,128)(2,1)}), bf16[1,3072,768]{2,1,0:T(8,128)(2,1)}) %all-gather.23.cloned.1.call-update) | async-done | bytes 4718608 | tf_op jit(solution)/shard_map/all_gather | solution.py:129
  292.4 6.6 fusion.81
  300.0 1.5 fusion.77
  301.7 5.1 fusion.82
  306.9 3.1 multiply_reduce_fusion
  310.6 1.2 copy-done.7
  311.8 1.7 convolution_convert_fusion
  313.5 1.4 copy.104
  314.9 1.1 reshape.203
  316.0 1.5 copy.105
  317.4 23.4 %all_to_all.63 = bf16[48,128,64]{1,2,0:T(8,128)(2,1)S(1)} all-to-all(bf16[48,128,64]{1,2,0:T(8,128)(2,1)S(1)} %bitcast.185), channel_id=1, replica_groups=mesh['dp'=8,'seq'=4] {'seq'}, dimensions={0} | all-to-all | bytes 1572864 | tf_op jit(solution)/shard_map/all_to_all | solution.py:276
  341.1 6.8 convolution_convert_fusion.3
  348.2 5.3 multiply_convert_fusion
  353.5 2.0 convolution_convert_fusion.4
  355.5 1.1 convolution_convert_fusion.1
  356.8 6.3 copy.113
  363.1 5.0 all-to-all-start.3
  368.1 2.2 fusion.46
  370.3 1.5 reshape.209
  371.9 5.3 convolution_bitcast_fusion.1
  377.2 5.9 copy.130
  383.0 5.3 fusion.64
  388.4 10.8 %reshape.211 = f32[2359296]{0:T(1024)} reshape(f32[3072,768]{1,0:T(8,128)} %fusion.64) | data formatting | bytes 18874368 | tf_op jit(solution)/shard_map/reshape | solution.py:335
  399.2 61.7 %all-to-all-done.3 = bf16[12,512,192]{2,0,1:T(8,128)(2,1)} async-done(((bf16[12,512,192]{2,0,1:T(8,128)(2,1)}), bf16[12,512,192]{2,0,1:T(8,128)(2,1)}, u32[]{:S(2)}, u32[]{:S(2)}) %all-to-all-start.3) | async-done | bytes 2359328 | tf_op jit(solution)/shard_map/all_to_all | solution.py:315
  460.8 6.1 copy.123
  466.9 2.2 copy.115
  469.1 2.2 copy.116
  471.4 1.4 copy-done.12
  472.8 4.9 convolution_bitcast_fusion
  477.7 8.0 copy.117
  485.7 7.9 reshape.208
  494.2 39.5 %all-reduce.20 = (f32[1536]{0:T(1024)S(1)}, f32[768]{0:T(1024)S(1)}, f32[768]{0:T(1024)S(1)}, f32[768]{0:T(1024)S(1)}, f32[3072]{0:T(1024)S(1)}, /*index=5*/f32[...) all-reduce(f32[1536]{0:T(1024)S(1)} %pad_maximum_fusion.2, ...), channel_id=15, replica_groups=mesh['dp'=8,'seq'=4] {'dp','seq'}, use_global_device_ids=true, to_apply=%region_14.15.clone | all-reduce | flops 9216 | bytes 73728
  538.4 6.2 add_convert_fusion
  544.6 377.2 %all-reduce.25.cloned.1.call-done = (f32[1769472]{0:T(1024)}, f32[589824]{0:T(1024)}, f32[2359296]{0:T(1024)}, f32[2359296]{0:T(1024)}) async-done(((f32[1769472]{0:T(1024)}, f32[589824]{0:T(1024)}, f32[2359296]{0:T(1024)}, f32[2359296]{0:T(1024)}), (f32[1769472]{0:T(1024)}, f32[589824]{0:T(1024)}, f32[2359296]{0:T(1024)}, f32[2359296]{0:T(1024)})) %all-reduce.25.cloned.1.call-update) | async-done | bytes 28311568
  921.9 0.9 dynamic-slice.2
  923.6 0.9 dynamic-slice.4
  925.1 1.0 dynamic-slice.8
  926.1 1.0 dynamic-slice.10
  (119 shorter events, 20.2 us)
Async XLA Ops:
  7.2 66.5 %all-gather.17.cloned.1.call-start = ((), (), s32[]{:S(2)}) async-start(), calls=%async_computation.4 | async-start | bytes 3649536 | tf_op jit(solution)/shard_map/all_gather | solution.py:121
  7.9 205.0 %all-gather.19.cloned.1.call-start = ((), (), s32[]{:S(2)}) async-start(), calls=%async_computation.5 | async-start | bytes 1216512 | tf_op jit(solution)/shard_map/all_gather | solution.py:123
  8.7 219.1 %all-gather.21.cloned.1.call-start = ((), (), s32[]{:S(2)}) async-start(), calls=%async_computation.6 | async-start | bytes 4866048 | tf_op jit(solution)/shard_map/all_gather | solution.py:127
  9.4 283.0 %all-gather.23.cloned.1.call-start = ((), (), s32[]{:S(2)}) async-start(), calls=%async_computation.7 | async-start | bytes 4866048 | tf_op jit(solution)/shard_map/all_gather | solution.py:129
  88.0 3.8 copy-start.16
  88.0 62.1 %all-to-all-start = ((bf16[48,128,192]{1,2,0:T(8,128)(2,1)}), bf16[48,128,192]{1,2,0:T(8,128)(2,1)S(1)}, u32[]{:S(2)}, u32[]{:S(2)}) async-start(bf16[48,128,192]{1,2,0:T(8,128)(2,1)} %bitcast.175), calls=%async_computation | async-start | bytes 4718592 | tf_op jit(solution)/shard_map/all_to_all | solution.py:158
  150.2 1.4 copy-start.1
  158.2 4.6 copy-start
  166.6 0.9 copy-start.10
  170.3 8.6 copy-start.2
  174.5 30.7 %all-to-all-start.1 = ((bf16[4,2,49152]{2,1,0:T(2,128)(2,1)}), bf16[4,2,49152]{2,1,0:T(2,128)(2,1)}, u32[]{:S(2)}, u32[]{:S(2)}) async-start(bf16[4,2,49152]{2,1,0:T(2,128)(2,1)} %reshape.271), calls=%async_computation.1 | async-start | bytes 1572864 | tf_op jit(solution)/shard_map/all_to_all | solution.py:179
  215.6 1.2 copy-start.5
  292.4 9.2 copy-start.18
  299.3 2.4 copy-start.13
  300.0 6.8 slice-start.3
  301.6 5.3 copy-start.3
  301.7 5.2 copy-start.6
  301.7 5.2 slice-start.4
  306.9 3.2 copy-start.17
  310.1 1.7 copy-start.14
  310.6 1.2 copy-start.7
  316.0 24.8 %copy-start.11 = (bf16[12,512,64]{1,2,0:T(8,128)(2,1)S(1)}, bf16[12,512,64]{1,2,0:T(8,128)(2,1)}, u32[]{:S(2)}) copy-start(bf16[12,512,64]{1,2,0:T(8,128)(2,1)} %copy-done.10) | copy-start | bytes 2359300
  316.0 32.0 %slice-start = ((s8[12582912]{0:T(1024)(128)(4,1)}), s8[4194304]{0:T(1024)(128)(4,1)S(1)}, s32[]{:S(2)}) async-start(s8[12582912]{0:T(1024)(128)(4,1)} %bitcast.163), calls=%async_computation.9 | async-start | bytes 8388608
  341.1 6.8 slice-start.1
  341.1 7.1 slice-start.2
  363.1 5.0 copy-start.9
  363.1 97.7 %all-to-all-start.3 = ((bf16[12,512,192]{2,0,1:T(8,128)(2,1)}), bf16[12,512,192]{2,0,1:T(8,128)(2,1)}, u32[]{:S(2)}, u32[]{:S(2)}) async-start(bf16[12,512,192]{2,0,1:T(8,128)(2,1)} %copy.113), calls=%async_computation.3 | async-start | bytes 8388608 | tf_op jit(solution)/shard_map/all_to_all | solution.py:315
  368.1 553.8 %all-reduce.25.cloned.1.call-start = ((), (), s32[]{:S(2)}) async-start(), calls=%async_computation.8 | async-start | bytes 56623104
  377.1 5.9 copy-start.4
  377.1 5.9 copy-start.8
  469.1 3.7 copy-start.15
  471.4 1.4 copy-start.12
Sparse Core Ops, SparseCore 0:
  10.8 62.8 all-gather.16
  76.5 79.1 all-gather.18
  158.5 69.2 all-gather.20
  230.5 61.8 all-gather.22
  493.8 428.0 all-reduce.24
where the time goes:
time: 943 us; the launch traced here: 935 us
  waiting for transfers between devices  607 us (64%)
  local copies, waits for them, and re-layouts  107 us (11%)
  blocking collectives  105 us (11%)
  matrix products  80.8 us (9%)
  between operations  14.6 us (2%)
  starting transfers between devices  13.3 us (1%)
    unnamed x6, waiting for transfers between devices  380 us
    unnamed x2, blocking collectives  82 us
    all_to_all x1, waiting for transfers between devices, per_device(): lax.all_to_all(d_mixed_heads, 'seq', split_axis=1, concat_axis=0, tiled=T...  61.7 us
    all_to_all x1, waiting for transfers between devices, per_device(): lax.all_to_all(to_heads(mixed, 3), 'seq', split_axis=0, concat_axis=1, ti...  58.2 us
    all_gather x1, waiting for transfers between devices, per_device(): lax.all_gather(down_weight[current], ('dp', 'seq'), axis=0, tiled=True)  56.2 us
    unnamed x74, local copies, waits for them, and re-layouts  32.9 us
    all_to_all x1, waiting for transfers between devices, per_device(): lax.all_to_all(context, 'seq', split_axis=1, concat_axis=0, tiled=True)  25.9 us
    all_to_all x1, blocking collectives, per_device(): lax.all_to_all(to_heads(d_context, 1), 'seq', split_axis=0, concat_axis=1...  23.4 us
  transfers between devices with their start and end apart: 8, of which 7 were waited for; matrix products, arithmetic and copies ran while one was open for 11% of the time, Pallas kernels for 0%

commit v1 on v0

--- a/solution.py
+++ b/solution.py
@@ -9,6 +9,7 @@
 
 NEG = -1e30
 EPS = 1e-05
+SENT = jnp.bfloat16
 
 
 def norm_rows(residual, gain_vec, shift_vec):
@@ -355,6 +356,228 @@
     return (output, input_grad) + stacked
 
 
+def split_cols(table, widths):
+    pieces, start = [], 0
+    for width in widths:
+        pieces.append(table[..., start : start + width])
+        start += width
+    return pieces
+
+
+def gather_rows(piece):
+    return lax.all_gather(
+        lax.all_gather(piece, "seq", axis=0, tiled=True), "dp", axis=0, tiled=True
+    )
+
+
+def scatter_rows(whole):
+    part = lax.psum_scatter(
+        whole.reshape(-1), ("dp", "seq"), scatter_dimension=0, tiled=True
+    )
+    return part.astype(jnp.float32).reshape((-1,) + whole.shape[1:])
+
+
+def per_sequence(
+    tokens,
+    cotangent,
+    lengths,
+    qkv_weight,
+    qv_bias,
+    out_weight,
+    out_bias,
+    norm_gain,
+    norm_shift,
+    up_weight,
+    up_bias,
+    down_weight,
+    down_bias,
+    final_gain,
+    final_shift,
+):
+    groups = lax.axis_size("seq")
+    ranks = lax.axis_size("dp") * groups
+    seq_here, tok_here, model_width = tokens.shape
+    own = seq_here // groups
+    key_count = tok_here * groups
+    head_dim = model_width // HEADS
+    row_count = own * key_count
+    score_scale = head_dim ** (-0.5)
+
+    def to_sequences(table):
+        return lax.all_to_all(table, "seq", split_axis=0, concat_axis=1, tiled=True)
+
+    def to_tokens(table):
+        return lax.all_to_all(
+            table.reshape(own, key_count, model_width),
+            "seq",
+            split_axis=1,
+            concat_axis=0,
+            tiled=True,
+        )
+
+    def heads_of(table):
+        return table.reshape(own, key_count, HEADS, head_dim).transpose(0, 2, 1, 3)
+
+    def flat_of(table):
+        return table.transpose(0, 2, 1, 3).reshape(row_count, model_width)
+
+    own_len = lax.dynamic_slice_in_dim(lengths, lax.axis_index("seq") * own, own, axis=0)
+    valid = jnp.arange(key_count, dtype=jnp.int32)[None, :] < own_len[:, None]
+
+    smalls = (
+        qv_bias[0],
+        out_bias[0],
+        norm_gain[0],
+        norm_shift[0],
+        up_bias[0],
+        down_bias[0],
+        final_gain[0],
+        final_shift[0],
+    )
+    widths = [item.shape[0] for item in smalls]
+    hid_half = to_sequences(tokens).reshape(row_count, model_width)
+    small_all = lax.all_gather(
+        jnp.concatenate(smalls), ("dp", "seq"), axis=0, tiled=True
+    ).reshape(ranks, -1)
+    mix_w = gather_rows(qkv_weight[0])
+    proj_w = gather_rows(out_weight[0])
+    upper_w = gather_rows(up_weight[0])
+    lower_w = gather_rows(down_weight[0])
+    mix_b, proj_b, gain_one, shift_one, upper_b, lower_b, gain_two, shift_two = [
+        item.reshape(-1).astype(jnp.float32) for item in split_cols(small_all, widths)
+    ]
+    grad = to_sequences(cotangent).reshape(row_count, model_width).astype(jnp.float32)
+
+    hidden = hid_half.astype(jnp.float32)
+    bias_full = jnp.concatenate(
+        [mix_b[:model_width], jnp.zeros((model_width,), jnp.float32), mix_b[model_width:]]
+    )
+    mixed = (matmul(hid_half, mix_w) + bias_full).astype(jnp.bfloat16)
+    queries = heads_of(mixed[:, :model_width])
+    keys_here = heads_of(mixed[:, model_width : 2 * model_width])
+    values = heads_of(mixed[:, 2 * model_width :])
+    scores = (
+        jnp.einsum("shqd,shkd->shqk", queries, keys_here, preferred_element_type=jnp.float32)
+        * score_scale
+    )
+    scores = jnp.where(valid[:, None, None, :], scores, NEG)
+    row_max = jnp.max(scores, axis=-1, keepdims=True)
+    log_total = row_max + jnp.log(jnp.sum(jnp.exp(scores - row_max), axis=-1, keepdims=True))
+    attn_probs = jnp.exp(scores - log_total)
+    probs_half = attn_probs.astype(jnp.bfloat16)
+    context = jnp.einsum(
+        "shqk,shkd->shqd", probs_half, values, preferred_element_type=jnp.float32
+    ).astype(jnp.bfloat16)
+    context_tok = flat_of(context)
+    first_norm, normed_one, inv_one = norm_rows(
+        hidden + matmul(context_tok, proj_w) + proj_b, gain_one, shift_one
+    )
+    first_half = first_norm.astype(jnp.bfloat16)
+    pre_act = matmul(first_half, upper_w) + upper_b
+    activated = gelu_exact(pre_act).astype(jnp.bfloat16)
+    last, normed_two, inv_two = norm_rows(
+        first_norm + matmul(activated, lower_w) + lower_b, gain_two, shift_two
+    )
+    output = to_tokens(last.astype(jnp.bfloat16))
+
+    d_gain_two = jnp.sum(grad * normed_two, axis=0)
+    d_shift_two = jnp.sum(grad, axis=0)
+    d_second = norm_back(grad, normed_two, inv_two, gain_two)
+    d_second_half = d_second.astype(jnp.bfloat16)
+    d_lower_b = jnp.sum(d_second, axis=0)
+    lower_part, d_second_half = lax.optimization_barrier(
+        (dot_rows(activated, d_second_half).astype(SENT), d_second_half)
+    )
+    d_lower_w = scatter_rows(lower_part)
+    d_pre = dot_back(d_second_half, lower_w) * gelu_slope(pre_act)
+    d_pre_half = d_pre.astype(jnp.bfloat16)
+    d_upper_b = jnp.sum(d_pre, axis=0)
+    upper_part, d_pre_half = lax.optimization_barrier(
+        (dot_rows(first_half, d_pre_half).astype(SENT), d_pre_half)
+    )
+    d_upper_w = scatter_rows(upper_part)
+    d_first = d_second + dot_back(d_pre_half, upper_w)
+    d_gain_one = jnp.sum(d_first * normed_one, axis=0)
+    d_shift_one = jnp.sum(d_first, axis=0)
+    d_resid = norm_back(d_first, normed_one, inv_one, gain_one)
+    d_resid_half = d_resid.astype(jnp.bfloat16)
+    d_proj_b = jnp.sum(d_resid, axis=0)
+    proj_part, d_resid_half = lax.optimization_barrier(
+        (dot_rows(context_tok, d_resid_half).astype(SENT), d_resid_half)
+    )
+    d_proj_w = scatter_rows(proj_part)
+    d_ctx_tok = dot_back(d_resid_half, proj_w).astype(jnp.bfloat16)
+    d_ctx = heads_of(d_ctx_tok)
+    d_values = jnp.einsum(
+        "shqk,shqd->shkd", probs_half, d_ctx, preferred_element_type=jnp.float32
+    ).astype(jnp.bfloat16)
+    d_probs = jnp.einsum("shqd,shkd->shqk", d_ctx, values, preferred_element_type=jnp.float32)
+    delta = jnp.sum(
+        d_ctx.astype(jnp.float32) * context.astype(jnp.float32), axis=-1, keepdims=True
+    )
+    d_scores = (attn_probs * (d_probs - delta) * score_scale).astype(jnp.bfloat16)
+    d_queries = jnp.einsum(
+        "shqk,shkd->shqd", d_scores, keys_here, preferred_element_type=jnp.float32
+    ).astype(jnp.bfloat16)
+    d_keys = jnp.einsum(
+        "shqk,shqd->shkd", d_scores, queries, preferred_element_type=jnp.float32
+    ).astype(jnp.bfloat16)
+    d_mixed = jnp.concatenate(
+        [flat_of(d_queries), flat_of(d_keys), flat_of(d_values)], axis=-1
+    )
+    col_sums = jnp.sum(d_mixed.astype(jnp.float32), axis=0)
+    d_mix_b = jnp.concatenate([col_sums[:model_width], col_sums[2 * model_width :]])
+    small_grads = jnp.concatenate(
+        [
+            item.reshape(ranks, -1)
+            for item in (
+                d_mix_b,
+                d_proj_b,
+                d_gain_one,
+                d_shift_one,
+                d_upper_b,
+                d_lower_b,
+                d_gain_two,
+                d_shift_two,
+            )
+        ],
+        axis=1,
+    )
+    d_mix_w = scatter_rows(dot_rows(hid_half, d_mixed).astype(SENT))
+    (
+        s_mix_b,
+        s_proj_b,
+        s_gain_one,
+        s_shift_one,
+        s_upper_b,
+        s_lower_b,
+        s_gain_two,
+        s_shift_two,
+    ) = split_cols(scatter_rows(small_grads)[0], widths)
+    input_grad = to_tokens((d_resid + dot_back(d_mixed, mix_w)).astype(jnp.bfloat16))
+    shares = (
+        d_mix_w,
+        s_mix_b,
+        d_proj_w,
+        s_proj_b,
+        s_gain_one,
+        s_shift_one,
+        d_upper_w,
+        s_upper_b,
+        d_lower_w,
+        s_lower_b,
+        s_gain_two,
+        s_shift_two,
+    )
+    return (output, input_grad) + tuple((item[None] for item in shares))
+
+
+def choose(*args):
+    if args[0].shape[0] % lax.axis_size("seq") == 0:
+        return per_sequence(*args)
+    return per_device(*args)
+
+
 def solution(mesh):
     placed = (
         P("dp", "seq", None),
@@ -374,7 +597,7 @@
         P(None, ("dp", "seq")),
     )
     return jax.shard_map(
-        per_device,
+        choose,
         mesh=mesh,
         in_specs=placed,
         out_specs=(

time: 943 us -> 579 us (0.61)
  waiting for transfers between devices: 607 us -> 210 us
  blocking collectives: 105 us -> 156 us
  local copies, waits for them, and re-layouts: 107 us -> 62.1 us
  other arithmetic: 7.81 us -> 35 us
    unnamed x6, waiting for transfers between devices: 380 us -> 172 us
    all_to_all x3 -> x4, waiting for transfers between devices: 146 us -> 37.4 us  [the longest x2 19.4 us: to_tokens(): lax.all_to_all(table.reshape(own, key_count, model_width), 'seq', split_a...]
    all_gather x4, waiting for transfers between devices: 81.3 us -> 0.03 us  [gather_rows(): lax.all_gather(lax.all_gather(piece, 'seq', axis=0, tiled=True), 'dp', ax...]
    all_gather x0 -> x4, blocking collectives: none -> 68.2 us  [gather_rows(): lax.all_gather(piece, 'seq', axis=0, tiled=True)]
    all_to_all x1 -> x0, blocking collectives: 23.4 us -> none  [per_device(): lax.all_to_all(to_heads(d_context, 1), 'seq', split_axis=0, concat_axis=1...]
    all_to_all x4 -> x0, local copies, waits for them, and re-layouts: 13.8 us -> none  [the longest x2 8.28 us: per_device(): lax.all_to_all(d_mixed_heads, 'seq', split_axis=1, concat_axis=0, tiled=T...]
    unnamed x74 -> x91, local copies, waits for them, and re-layouts: 32.9 us -> 20.3 us
    unnamed x2 -> x6, other arithmetic: 0.01 us -> 10.9 us
  transfers between devices with their start and end apart: 8 -> 9, of which waited for: 7 -> 3; matrix products, arithmetic and copies ran while one was open for 11% -> 13% of each run, Pallas kernels for 0% -> 0%
where the time goes in v1:
time: 579 us; the launch traced here: 567 us
  waiting for transfers between devices  210 us (36%)
  blocking collectives  156 us (27%)
  matrix products  74.1 us (13%)
  local copies, waits for them, and re-layouts  62.1 us (11%)
  other arithmetic  35 us (6%)
  starting transfers between devices  15.5 us (3%)
  between operations  14.9 us (3%)
    unnamed x6, waiting for transfers between devices  172 us
    unnamed x2, blocking collectives  87.8 us
    all_gather x4, blocking collectives, gather_rows(): lax.all_gather(piece, 'seq', axis=0, tiled=True)  68.2 us
    dot_general x4, matrix products, matmul(): return jnp.dot(left, right, preferred_element_type=jnp.float32)  21.9 us
    unnamed x91, local copies, waits for them, and re-layouts  20.3 us
    all_to_all x2, waiting for transfers between devices, to_tokens(): lax.all_to_all(table.reshape(own, key_count, model_width), 'seq', split_a...  19.4 us
    reshape x4, local copies, waits for them, and re-layouts, scatter_rows(): whole.reshape(-1)  18.7 us
    all_to_all x2, waiting for transfers between devices, to_sequences(): return lax.all_to_all(table, 'seq', split_axis=0, concat_axis=1, tiled=True)  17.9 us
  transfers between devices with their start and end apart: 9, of which 3 were waited for; matrix products, arithmetic and copies ran while one was open for 13% of the time, Pallas kernels for 0%

profile of v1, /device:TPU:0, one launch (start us, length us, event | category | flops | bytes accessed | tf_op | source)
XLA Modules:
  0.0 567.1 jit_solution(4840916332587480258)
XLA Ops:
  7.3 18.5 %all-gather = bf16[1,96,2304]{2,1,0:T(8,128)(2,1)} all-gather(bf16[1,24,2304]{2,1,0:T(8,128)(2,1)} %param.18), channel_id=2, replica_groups=mesh['dp'=8,'seq'=4] {'seq'}, dimensions={1}, use_global_device_ids=true | all-gather | bytes 552960 | tf_op jit(solution)/shard_map/all_gather | solution.py:369
  25.9 14.5 %all-gather.2 = bf16[1,96,768]{2,1,0:T(8,128)(2,1)} all-gather(bf16[1,24,768]{2,1,0:T(8,128)(2,1)} %param.20), channel_id=4, replica_groups=mesh['dp'=8,'seq'=4] {'seq'}, dimensions={1}, use_global_device_ids=true | all-gather | bytes 184320 | tf_op jit(solution)/shard_map/all_gather | solution.py:369
  40.4 17.7 %all-gather.4 = bf16[1,96,3072]{2,1,0:T(8,128)(2,1)} all-gather(bf16[1,24,3072]{2,1,0:T(8,128)(2,1)} %param.24), channel_id=6, replica_groups=mesh['dp'=8,'seq'=4] {'seq'}, dimensions={1}, use_global_device_ids=true | all-gather | bytes 737280 | tf_op jit(solution)/shard_map/all_gather | solution.py:369
  58.2 17.5 %all-gather.6 = bf16[1,384,768]{2,1,0:T(8,128)(2,1)} all-gather(bf16[1,96,768]{2,1,0:T(8,128)(2,1)} %param.26), channel_id=8, replica_groups=mesh['dp'=8,'seq'=4] {'seq'}, dimensions={1}, use_global_device_ids=true | all-gather | bytes 737280 | tf_op jit(solution)/shard_map/all_gather | solution.py:369
  75.7 3.8 all-to-all-start.2
  79.9 41.5 %all-reduce = bf16[9216]{0:T(1024)(128)(2,1)S(1)} all-reduce(bf16[9216]{0:T(1024)(128)(2,1)S(1)} %dynamic-update-slice), channel_id=1, replica_groups=mesh['dp'=8,'seq'=4] {'dp','seq'}, use_global_device_ids=true, to_apply=%add | all-reduce | flops 9216 | bytes 36864
  121.6 3.6 all-to-all-start
  127.7 17.9 %all-to-all-done = bf16[4,128,768]{2,1,0:T(8,128)(2,1)S(1)} async-done(((bf16[4,128,768]{2,1,0:T(8,128)(2,1)}), bf16[4,128,768]{2,1,0:T(8,128)(2,1)S(1)}, u32[]{:S(2)}, u32[]{:S(2)}) %all-to-all-start) | async-done | bytes 786464 | tf_op jit(solution)/shard_map/all_to_all | solution.py:407
  145.7 4.3 fusion.14
  150.0 1.3 fusion.46
  151.5 1.7 copy.61
  153.2 2.3 copy.62
  155.5 3.1 fusion.1
  158.6 2.6 exponential_reduce_fusion
  161.2 1.9 copy-done
  163.2 10.0 %fusion = bf16[12,512,512]{1,2,0:T(8,128)(2,1)} fusion(f32[12,512,512]{1,2,0:T(8,128)} %copy-done, f32[12,512]{1,0:T(8,128)S(1)} %log_add_fusion, pred[512]{0:T(512)(128)(4,1)S(1)} %iota_compare_fusion), kind=kLoop, calls=%fused_computation.4 | loop fusion | flops 12582912 | bytes 18899456 | tf_op jit(solution)/shard_map/convert_element_type | solution.py:467
  173.2 5.2 convolution_convert_fusion.6
  178.5 2.6 fusion.49
  181.1 1.2 copy-done.8
  182.6 8.5 %multiply_convert_fusion.1 = (bf16[512,3072]{1,0:T(8,128)(2,1)}, f32[512,3072]{1,0:T(8,128)}) fusion(f32[3072]{0:T(1024)S(1)} %reshape.366, bf16[1,768,3072]{2,1,0:T(8,128)(2,1)} %all-gather.17.cloned.1.call-done, f32[512,768]{1,0:T(8,128)} %copy-done.8, f32[768]{0:T(1024)S(1)} %reshape.365, f32[768]{0:T(1024)S(1)} %reshape.364, ...), kind=kOutput, calls=%fused_computation.12 | convolution fusion | flops 2427322368 | bytes 15751168 | tf_op jit(solution)/shard_map/dot_general | solution.py:43
  191.1 6.5 %fusion.50 = (f32[512]{0:T(512)S(1)}, f32[512,768]{1,0:T(8,128)S(1)}) fusion(f32[768]{0:T(1024)S(1)} %reshape.367, bf16[512,3072]{1,0:T(8,128)(2,1)} %get-tuple-element.68, bf16[1,3072,768]{2,1,0:T(8,128)(2,1)} %all-gather.19.cloned.1.call-done, f32[768]{0:T(1024)S(1)} %reshape.365, f32[768]{0:T(1024)S(1)} %reshape.364, f32[512]{0:T(512)S(1)} %add_rsqrt_fusion.1, ...), kind=kOutput, calls=%fused_computation.108 | convolution fusion | flops 2418671104 | bytes 11025408 | tf_op jit(solution)/shard_map/dot_general | solution.py:43
  198.6 1.6 fusion.42
  200.3 4.4 convolution_convert_fusion.2
  204.8 5.3 fusion.45
  210.1 5.0 convolution_convert_fusion.1
  215.2 3.6 multiply_reduce_fusion
  219.9 1.8 convolution_convert_fusion.3
  221.7 1.7 convolution_convert_fusion.4
  223.4 2.5 copy.65
  225.9 1.6 multiply_reduce_fusion.1
  227.5 8.4 %multiply_convert_fusion = bf16[12,512,512]{1,2,0:T(8,128)(2,1)S(1)} fusion(f32[12,512,512]{1,2,0:T(8,128)} %copy-done, f32[12,512]{1,0:T(8,128)S(1)} %multiply_reduce_fusion.1, f32[12,512]{1,0:T(8,128)S(1)} %log_add_fusion, pred[512]{0:T(512)(128)(4,1)S(1)} %iota_compare_fusion, bf16[12,512,64]{1,2,0:T(8,128)(2,1)} %bitcast.173, ...), kind=kOutput, calls=%fused_computation | convolution fusion | flops 424673280 | bytes 20496896 | tf_op jit(solution)/shard_map/shqd,shkd->shqk/dot_general | solution.py:514
  235.9 1.1 convolution_convert_fusion.5
  237.1 2.0 convolution_convert_fusion.8
  239.1 2.0 convolution_convert_fusion.7
  241.2 0.9 copy-done.15
  242.0 3.7 fusion.15
  245.7 4.5 copy.71
  250.3 5.7 %reshape.351 = bf16[1769472]{0:T(1024)(128)(2,1)} reshape(bf16[768,2304]{1,0:T(8,128)(2,1)S(1)} %copy.71) | data formatting | bytes 7077888 | tf_op jit(solution)/shard_map/reshape | solution.py:375
  255.9 3.3 reshape.360
  259.3 5.9 %copy.79 = bf16[96,24,8,128]{3,1,2,0:T(8,128)(2,1)} copy(bf16[96,24,8,128]{3,2,1,0:T(8,128)(2,1)} %bitcast.186) | data formatting | bytes 9437184
  265.1 9.6 %reshape.362 = bf16[2359296]{0:T(1024)(128)(2,1)} reshape(bf16[3072,768]{1,0:T(8,128)(2,1)} %convolution_convert_fusion.2) | data formatting | bytes 9437184 | tf_op jit(solution)/shard_map/reshape | solution.py:375
  274.8 1.1 copy-done.7
  276.6 4.8 fusion.34
  281.4 1.2 copy.82
  283.2 5.4 reduce.13
  288.6 1.0 reshape.387
  289.6 4.4 all-to-all-start.3
  294.1 2.4 copy.83
  296.5 5.4 reduce.12
  302.0 1.0 reshape.385
  302.9 19.4 %all-to-all-done.3 = bf16[4,2,49152]{2,1,0:T(2,128)(2,1)} async-done(((bf16[4,2,49152]{2,1,0:T(2,128)(2,1)}), bf16[4,2,49152]{2,1,0:T(2,128)(2,1)}, u32[]{:S(2)}, u32[]{:S(2)}) %all-to-all-start.3) | async-done | bytes 786464 | tf_op jit(solution)/shard_map/all_to_all | solution.py:410
  322.4 3.6 all-to-all-start.1
  326.0 1.5 convert_reduce_fusion
  328.5 46.3 %all-reduce.2 = f32[9216]{0:T(1024)S(1)} all-reduce(f32[9216]{0:T(1024)S(1)} %reshape.359), channel_id=11, replica_groups=mesh['dp'=8,'seq'=4] {'dp','seq'}, use_global_device_ids=true, to_apply=%region_20.21.clone | all-reduce | flops 9216 | bytes 73728
  376.6 2.4 reshape.388
  379.0 1.0 copy.78
  380.8 1.0 copy.77
  381.8 172.2 %all-reduce.9.cloned.1.call-done = (bf16[1769472]{0:T(1024)(128)(2,1)}, bf16[589824]{0:T(1024)(128)(2,1)}, bf16[2359296]{0:T(1024)(128)(2,1)}, bf16[2359296]{0:T(1024)(128)(2,1)}) async-done(((bf16[1769472]{0:T(1024)(128)(2,1)}, bf16[589824]{0:T(1024)(128)(2,1)}, bf16[2359296]{0:T(1024)(128)(2,1)}, bf16[2359296]{0:T(1024)(128)(2,1)}), (bf16[1769472]{0:T(1024)(128)(2,1)}, bf16[589824]{0:T(1024)(128)(2,1)}, ...) | async-done | bytes 14155792
  554.0 0.9 dynamic-slice_convert_fusion.1
  554.9 0.8 reshape.373
  555.7 0.9 dynamic-slice_convert_fusion
  556.6 0.8 reshape.374
  557.4 0.9 dynamic-slice_convert_fusion.2
  559.0 0.8 dynamic-slice_convert_fusion.3
  (154 shorter events, 12.2 us)
Async XLA Ops:
  7.2 72.3 %copy-start.28 = (bf16[1,24]{1,0:T(2,128)(2,1)S(1)}, bf16[1,24]{1,0:T(2,128)(2,1)}, u32[]{:S(2)}) copy-start(bf16[1,24]{1,0:T(2,128)(2,1)} %param.29) | copy-start | bytes 148
  7.2 72.3 %copy-start.21 = (bf16[1,48]{1,0:T(2,128)(2,1)S(1)}, bf16[1,48]{1,0:T(2,128)(2,1)}, u32[]{:S(2)}) copy-start(bf16[1,48]{1,0:T(2,128)(2,1)} %param.19) | copy-start | bytes 292
  7.2 72.3 %copy-start.22 = (bf16[1,24]{1,0:T(2,128)(2,1)S(1)}, bf16[1,24]{1,0:T(2,128)(2,1)}, u32[]{:S(2)}) copy-start(bf16[1,24]{1,0:T(2,128)(2,1)} %param.21) | copy-start | bytes 148
  7.2 72.3 %copy-start.23 = (bf16[1,24]{1,0:T(2,128)(2,1)S(1)}, bf16[1,24]{1,0:T(2,128)(2,1)}, u32[]{:S(2)}) copy-start(bf16[1,24]{1,0:T(2,128)(2,1)} %param.22) | copy-start | bytes 148
  7.2 72.3 %copy-start.24 = (bf16[1,24]{1,0:T(2,128)(2,1)S(1)}, bf16[1,24]{1,0:T(2,128)(2,1)}, u32[]{:S(2)}) copy-start(bf16[1,24]{1,0:T(2,128)(2,1)} %param.23) | copy-start | bytes 148
  7.2 72.3 %copy-start.25 = (bf16[1,96]{1,0:T(2,128)(2,1)S(1)}, bf16[1,96]{1,0:T(2,128)(2,1)}, u32[]{:S(2)}) copy-start(bf16[1,96]{1,0:T(2,128)(2,1)} %param.25) | copy-start | bytes 580
  7.2 72.3 %copy-start.26 = (bf16[1,24]{1,0:T(2,128)(2,1)S(1)}, bf16[1,24]{1,0:T(2,128)(2,1)}, u32[]{:S(2)}) copy-start(bf16[1,24]{1,0:T(2,128)(2,1)} %param.27) | copy-start | bytes 148
  7.3 72.3 %copy-start.27 = (bf16[1,24]{1,0:T(2,128)(2,1)S(1)}, bf16[1,24]{1,0:T(2,128)(2,1)}, u32[]{:S(2)}) copy-start(bf16[1,24]{1,0:T(2,128)(2,1)} %param.28) | copy-start | bytes 148
  7.3 138.4 %all-gather.13.cloned.1.call-start = ((), (), s32[]{:S(2)}) async-start(), calls=%async_computation.4 | async-start | bytes 3981312 | tf_op jit(solution)/shard_map/all_gather | solution.py:368
  25.8 152.6 %all-gather.15.cloned.1.call-start = ((), (), s32[]{:S(2)}) async-start(), calls=%async_computation.5 | async-start | bytes 1327104 | tf_op jit(solution)/shard_map/all_gather | solution.py:368
  40.4 85.7 %copy-start.30 = (s32[4]{0:T(128)S(1)}, s32[4]{0:T(128)}, u32[]{:S(2)}) copy-start(s32[4]{0:T(128)} %param.17) | copy-start | bytes 52
  40.4 142.2 %all-gather.17.cloned.1.call-start = ((), (), s32[]{:S(2)}) async-start(), calls=%async_computation.6 | async-start | bytes 5308416 | tf_op jit(solution)/shard_map/all_gather | solution.py:368
  58.2 133.0 %all-gather.19.cloned.1.call-start = ((), (), s32[]{:S(2)}) async-start(), calls=%async_computation.7 | async-start | bytes 5308416 | tf_op jit(solution)/shard_map/all_gather | solution.py:368
  75.7 45.8 %all-to-all-start.2 = ((bf16[4,128,768]{2,1,0:T(8,128)(2,1)}), bf16[4,128,768]{2,1,0:T(8,128)(2,1)S(1)}, u32[]{:S(2)}, u32[]{:S(2)}) async-start(bf16[4,128,768]{2,1,0:T(8,128)(2,1)} %param.16), calls=%async_computation.2 | async-start | bytes 1572864 | tf_op jit(solution)/shard_map/all_to_all | solution.py:407
  121.6 24.1 %all-to-all-start = ((bf16[4,128,768]{2,1,0:T(8,128)(2,1)}), bf16[4,128,768]{2,1,0:T(8,128)(2,1)S(1)}, u32[]{:S(2)}, u32[]{:S(2)}) async-start(bf16[4,128,768]{2,1,0:T(8,128)(2,1)} %param.15), calls=%async_computation | async-start | bytes 1572864 | tf_op jit(solution)/shard_map/all_to_all | solution.py:407
  125.2 428.8 %all-reduce.9.cloned.1.call-start = ((), (), s32[]{:S(2)}) async-start(), calls=%async_computation.8 | async-start | bytes 28311552
  145.6 4.3 copy-start.16
  151.5 7.1 %copy-start.1 = (bf16[512,768]{0,1:T(8,128)(2,1)}, bf16[512,768]{0,1:T(8,128)(2,1)S(1)}, u32[]{:S(2)}) copy-start(bf16[512,768]{0,1:T(8,128)(2,1)S(1)} %copy.60) | copy-start | bytes 2359300
  158.6 4.5 copy-start
  163.2 10.1 %copy-start.4 = (bf16[512,768]{0,1:T(8,128)(2,1)S(1)}, bf16[512,768]{0,1:T(8,128)(2,1)}, u32[]{:S(2)}) copy-start(bf16[512,768]{0,1:T(8,128)(2,1)} %copy.62) | copy-start | bytes 2359300
  181.1 1.2 copy-start.8
  197.9 2.4 copy-start.31
  198.6 6.1 %slice-start.6 = ((s8[6291456]{0:T(1024)(128)(4,1)}), s8[4194304]{0:T(1024)(128)(4,1)S(1)}, s32[]{:S(2)}) async-start(s8[6291456]{0:T(1024)(128)(4,1)} %bitcast.210), calls=%async_computation.15 | async-start | bytes 8388608
  200.2 4.5 slice-start.4
  200.3 4.5 slice-start.5
  200.3 4.5 slice-start.7
  200.3 14.8 %slice-start.2 = ((s8[4718592]{0:T(1024)(128)(4,1)}), s8[4194304]{0:T(1024)(128)(4,1)S(1)}, s32[]{:S(2)}) async-start(s8[4718592]{0:T(1024)(128)(4,1)} %bitcast.206), calls=%async_computation.11 | async-start | bytes 8388608
  204.8 5.3 copy-start.9
  204.8 10.3 %slice-start.3 = ((s8[4718592]{0:T(1024)(128)(4,1)}), s8[524288]{0:T(1024)(128)(4,1)S(1)}, s32[]{:S(2)}) async-start(s8[4718592]{0:T(1024)(128)(4,1)} %bitcast.206), calls=%async_computation.12 | async-start | bytes 1048576
  218.8 1.1 copy-start.5
  219.3 2.4 copy-start.10
  219.3 2.4 copy-start.29
  223.4 15.7 %slice-start = ((s8[6291456]{0:T(1024)(128)(4,1)}), s8[2097152]{0:T(1024)(128)(4,1)S(1)}, s32[]{:S(2)}) async-start(s8[6291456]{0:T(1024)(128)(4,1)} %bitcast.165), calls=%async_computation.9 | async-start | bytes 4194304
  227.5 11.6 %slice-start.1 = ((s8[6291456]{0:T(1024)(128)(4,1)}), s8[4194304]{0:T(1024)(128)(4,1)S(1)}, s32[]{:S(2)}) async-start(s8[6291456]{0:T(1024)(128)(4,1)} %bitcast.165), calls=%async_computation.10 | async-start | bytes 8388608
  235.9 1.1 copy-start.2
  237.1 4.1 copy-start.6
  237.1 2.0 copy-start.3
  239.1 2.0 copy-start.12
  239.1 2.9 copy-start.17
  241.1 0.9 copy-start.15
  274.8 1.1 copy-start.7
  274.8 1.6 copy-start.11
  274.8 1.8 copy-start.13
  289.6 32.8 %all-to-all-start.3 = ((bf16[4,2,49152]{2,1,0:T(2,128)(2,1)}), bf16[4,2,49152]{2,1,0:T(2,128)(2,1)}, u32[]{:S(2)}, u32[]{:S(2)}) async-start(bf16[4,2,49152]{2,1,0:T(2,128)(2,1)} %reshape.387), calls=%async_computation.3 | async-start | bytes 1572864 | tf_op jit(solution)/shard_map/all_to_all | solution.py:410
  301.9 24.1 %copy-start.14 = (bf16[12,512,64]{1,2,0:T(8,128)(2,1)S(1)}, bf16[12,512,64]{1,2,0:T(8,128)(2,1)}, u32[]{:S(2)}) copy-start(bf16[12,512,64]{1,2,0:T(8,128)(2,1)} %copy-done.12) | copy-start | bytes 2359300
  301.9 25.9 %copy-start.20 = (f32[768]{0:T(1024)S(1)}, f32[768]{0:T(1024)}, u32[]{:S(2)}) copy-start(f32[768]{0:T(1024)} %get-tuple-element.26) | copy-start | bytes 9220
  301.9 26.0 %copy-start.19 = (f32[768]{0:T(1024)S(1)}, f32[768]{0:T(1024)}, u32[]{:S(2)}) copy-start(f32[768]{0:T(1024)} %get-tuple-element.31) | copy-start | bytes 9220
  301.9 26.1 %copy-start.18 = (f32[3072]{0:T(1024)S(1)}, f32[3072]{0:T(1024)}, u32[]{:S(2)}) copy-start(f32[3072]{0:T(1024)} %get-tuple-element.42) | copy-start | bytes 36868
  322.4 57.7 %all-to-all-start.1 = ((bf16[4,2,49152]{2,1,0:T(2,128)(2,1)}), bf16[4,2,49152]{2,1,0:T(2,128)(2,1)S(1)}, u32[]{:S(2)}, u32[]{:S(2)}) async-start(bf16[4,2,49152]{2,1,0:T(2,128)(2,1)} %reshape.385), calls=%async_computation.1 | async-start | bytes 1572864 | tf_op jit(solution)/shard_map/all_to_all | solution.py:410
Sparse Core Ops, SparseCore 0:
  25.9 33.8 all-gather.12
  61.7 23.9 all-gather.14
  87.5 39.4 all-gather.16
  128.7 38.7 all-gather.18
  274.9 278.9 all-reduce.8
